TPU v7x, 512 devices: a whole 4x8x8 slice. The times are simulated.
512 devices in a mesh: seq: 32 (over x, y), head: 16 (over z, core).
Axes of the slice: x: 4, y: 8, z: 8, core: 2. Of those that a mesh axis runs over, the one named last changes fastest.
Arguments:
- queries: bfloat16 [65536, 2048], P(('seq', 'head')), may hold values from -6 to 6
- keys: bfloat16 [65536, 2048], P(('seq', 'head')), may hold values from -6 to 6
- values: bfloat16 [65536, 2048], P(('seq', 'head')), may hold values from -6 to 6
- log_decay: bfloat16 [65536, 16], P(('seq', 'head')), may hold values from -0.6 to 0, as said below
- out_weight: bfloat16 [2048, 2048], P(('seq', 'head')), may hold values from -0.125 to 0.125
Outputs:
- mixed_out: bfloat16 [65536, 2048], P(('seq', 'head'))
Inputs may be any that keep to these rules, and one draw needn't show every extreme that they name: `log_decay`: every entry is at most zero.
All inputs are finite; a program needn't handle non-finite values.
Results may differ from a plain program's by a relative error of at most 0.0054.
Values may be sent and summed in bfloat16 or wider, within the bound.
No kernel may reach another device: no remote copies, remote signals or barrier semaphores. Data moves between devices by JAX's collectives and lax.ppermute only.
A program may use at most 64 MiB of HBM per device.

v0:
```python
import jax
import jax.numpy as jnp
from jax import lax
from jax.sharding import PartitionSpec as P

SPAN = 256


def entering(x, axis, combine, identity):
    count, place = (lax.axis_size(axis), lax.axis_index(axis))
    everything = jax.tree.map(lambda part: lax.all_gather(part, axis), x)
    start = jax.tree.map(
        lambda part, zero: jnp.broadcast_to(jnp.asarray(zero, part.dtype), part.shape), x, identity
    )

    def turn(k, before):
        reached = k < place
        new = combine(before, jax.tree.map(lambda part: part[k], everything))
        return jax.tree.map(lambda a, b: jnp.where(reached, a, b), new, before)

    return lax.fori_loop(0, count, turn, start)


def local(queries, keys, values, log_decay, out_weight):
    queries_loc, keys_loc, values_loc, decay_loc = (
        lax.all_to_all(queries, "head", split_axis=1, concat_axis=0, tiled=True),
        lax.all_to_all(keys, "head", split_axis=1, concat_axis=0, tiled=True),
        lax.all_to_all(values, "head", split_axis=1, concat_axis=0, tiled=True),
        lax.all_to_all(log_decay, "head", split_axis=1, concat_axis=0, tiled=True),
    )
    shard_rows = queries_loc.shape[0]
    head_count = decay_loc.shape[1]
    head_dim = queries_loc.shape[1] // head_count
    block_count = shard_rows // SPAN
    queries_blk = queries_loc.reshape(block_count, SPAN, head_count, head_dim)
    keys_blk = keys_loc.reshape(block_count, SPAN, head_count, head_dim)
    values_blk = values_loc.reshape(block_count, SPAN, head_count, head_dim)
    within = jnp.cumsum(
        decay_loc.reshape(block_count, SPAN, head_count).astype(jnp.float32), axis=1
    )
    block_decay = within[:, -1, :]
    within_t = jnp.transpose(within, (0, 2, 1))
    causal = lax.broadcasted_iota(jnp.int32, (SPAN, SPAN), 0) >= lax.broadcasted_iota(
        jnp.int32, (SPAN, SPAN), 1
    )
    differences = within_t[:, :, :, None] - within_t[:, :, None, :]
    decay_mask = jnp.exp(jnp.where(causal[None, None], differences, -jnp.inf))
    scores = jnp.einsum(
        "nthd,nshd->nhts", queries_blk, keys_blk, preferred_element_type=jnp.float32
    )
    weights = (scores * decay_mask).astype(jnp.bfloat16)
    local_part = jnp.einsum(
        "nhts,nshd->nthd", weights, values_blk, preferred_element_type=jnp.float32
    )
    scaled_keys = (
        jnp.exp(block_decay[:, None, :] - within)[..., None] * keys_blk.astype(jnp.float32)
    ).astype(jnp.bfloat16)
    block_state = jnp.einsum(
        "nshd,nshe->nhde", scaled_keys, values_blk, preferred_element_type=jnp.float32
    )
    decay_incl = jnp.cumsum(block_decay, axis=0)
    decay_excl = decay_incl - block_decay
    block_index = lax.broadcasted_iota(jnp.int32, (block_count, block_count), 0)
    earlier_blocks = block_index > lax.broadcasted_iota(jnp.int32, (block_count, block_count), 1)
    pair_gaps = decay_excl[:, None, :] - decay_incl[None, :, :]
    block_weights = jnp.exp(jnp.where(earlier_blocks[:, :, None], pair_gaps, -jnp.inf))
    prior_states = jnp.einsum(
        "cjh,jhde->chde", block_weights, block_state, precision=lax.Precision.HIGHEST
    )
    total_decay = decay_incl[-1]
    final_state = jnp.einsum(
        "jh,jhde->hde",
        jnp.exp(total_decay[None, :] - decay_incl),
        block_state,
        precision=lax.Precision.HIGHEST,
    )

    def link(earlier, later):
        return (jnp.exp(later[1])[:, None, None] * earlier[0] + later[0], earlier[1] + later[1])

    incoming, _ = entering(
        (final_state, total_decay),
        "seq",
        link,
        (jnp.zeros_like(final_state), jnp.zeros_like(total_decay)),
    )
    full_states = prior_states + jnp.exp(decay_excl)[:, :, None, None] * incoming[None]
    scaled_queries = queries_blk.astype(jnp.float32) * jnp.exp(within)[..., None]
    carried_part = jnp.einsum(
        "nthd,nhde->nthe", scaled_queries, full_states, precision=lax.Precision.HIGHEST
    )
    combined = local_part + carried_part
    normed = (
        combined * lax.rsqrt(jnp.mean(combined * combined, axis=-1, keepdims=True) + 1e-05)
    ).astype(jnp.bfloat16)
    normed = normed.reshape(shard_rows, head_count * head_dim)
    restored = lax.all_to_all(normed, "head", split_axis=0, concat_axis=1, tiled=True)
    projected = jnp.dot(
        restored,
        lax.all_gather(out_weight, ("seq", "head"), axis=0, tiled=True),
        preferred_element_type=jnp.float32,
    )
    return projected.astype(jnp.bfloat16)


def solution(mesh):
    placed = (
        P(("seq", "head"), None),
        P(("seq", "head"), None),
        P(("seq", "head"), None),
        P(("seq", "head"), None),
        P(("seq", "head"), None),
    )
    return jax.shard_map(
        local, mesh=mesh, in_specs=placed, out_specs=P(("seq", "head"), None), check_vma=False
    )
```

profile of v0, /device:TPU:1, one launch (start us, length us, event | category | flops | bytes accessed | tf_op | source)
XLA Modules:
  0.0 307.7 jit_solution(8402958771548732288)
XLA Ops:
  7.9 11.8 %all-to-all-start.2 = ((bf16[128,16,1]{0,2,1:T(2,128)(2,1)}), bf16[128,16,1]{0,2,1:T(2,128)(2,1)S(1)}, u32[]{:S(2)}, u32[]{:S(2)}) async-start(bf16[128,16,1]{0,2,1:T(2,128)(2,1)} %copy.47), calls=%async_computation.2 | async-start | bytes 16384 | tf_op jit(solution)/shard_map/all_to_all | solution.py:29
  19.7 2.0 copy.45
  21.7 4.9 %all-to-all-done.2 = bf16[128,16,1]{0,2,1:T(2,128)(2,1)S(1)} async-done(((bf16[128,16,1]{0,2,1:T(2,128)(2,1)}), bf16[128,16,1]{0,2,1:T(2,128)(2,1)S(1)}, u32[]{:S(2)}, u32[]{:S(2)}) %all-to-all-start.2) | async-done | bytes 4128 | tf_op jit(solution)/shard_map/all_to_all | solution.py:29
  26.7 4.0 %all-to-all-start.1 = ((bf16[128,16,128]{0,2,1:T(8,128)(2,1)}), bf16[128,16,128]{0,2,1:T(8,128)(2,1)S(1)}, u32[]{:S(2)}, u32[]{:S(2)}) async-start(bf16[128,16,128]{0,2,1:T(8,128)(2,1)} %bitcast.2), calls=%async_computation.1 | async-start | bytes 1048576 | tf_op jit(solution)/shard_map/all_to_all | solution.py:27
  32.4 15.6 %all-to-all-done.1 = bf16[128,16,128]{0,2,1:T(8,128)(2,1)S(1)} async-done(((bf16[128,16,128]{0,2,1:T(8,128)(2,1)}), bf16[128,16,128]{0,2,1:T(8,128)(2,1)S(1)}, u32[]{:S(2)}, u32[]{:S(2)}) %all-to-all-start.1) | async-done | bytes 524320 | tf_op jit(solution)/shard_map/all_to_all | solution.py:27
  48.0 3.5 %all-to-all-start.3 = ((bf16[128,16,128]{2,0,1:T(8,128)(2,1)}), bf16[128,16,128]{2,0,1:T(8,128)(2,1)S(1)}, u32[]{:S(2)}, u32[]{:S(2)}) async-start(bf16[128,16,128]{2,0,1:T(8,128)(2,1)} %copy_bitcast_fusion), calls=%async_computation.3 | async-start | bytes 1048576 | tf_op jit(solution)/shard_map/all_to_all | solution.py:28
  53.0 15.1 %all-to-all-done.3 = bf16[128,16,128]{2,0,1:T(8,128)(2,1)S(1)} async-done(((bf16[128,16,128]{2,0,1:T(8,128)(2,1)}), bf16[128,16,128]{2,0,1:T(8,128)(2,1)S(1)}, u32[]{:S(2)}, u32[]{:S(2)}) %all-to-all-start.3) | async-done | bytes 524320 | tf_op jit(solution)/shard_map/all_to_all | solution.py:28
  68.9 2.0 fusion.18
  72.6 3.5 %all-to-all-start = ((bf16[128,16,128]{2,0,1:T(8,128)(2,1)}), bf16[128,16,128]{2,0,1:T(8,128)(2,1)S(1)}, u32[]{:S(2)}, u32[]{:S(2)}) async-start(bf16[128,16,128]{2,0,1:T(8,128)(2,1)} %copy_bitcast_fusion.1), calls=%async_computation | async-start | bytes 1048576 | tf_op jit(solution)/shard_map/all_to_all | solution.py:26
  78.7 61.9 %all-reduce = f32[32]{0:T(128)S(1)} all-reduce(f32[32]{0:T(128)S(1)} %bitcast_dynamic-update-slice_fusion), channel_id=1, replica_groups=mesh['seq'=32,'head'=16] {'seq'}, use_global_device_ids=true, to_apply=%add | all-reduce | flops 32 | bytes 256
  140.8 5.6 %all-gather.5.cloned.1.call-done = f32[4096,128]{1,0:T(8,128)} async-done(((f32[128,128]{1,0:T(8,128)}), f32[4096,128]{1,0:T(8,128)}) %all-gather.5.cloned.1.call-update) | async-done | bytes 2097168 | tf_op jit(solution)/shard_map/all_gather | solution.py:11
  146.4 64.9 %while.14 = (s32[]{:T(128)}, f32[1,128,128]{2,1,0:T(8,128)S(1)}, s32[]{:T(128)}, f32[32,1]{0,1:T(1,128)S(1)}, f32[32,1,128,128]{3,2,1,0:T(8,128)}, /*index=5*/s32[]{:T(128)}, s32[]{:T(128)}) while((s32[]{:T(128)}, f32[1,128,128]{2,1,0:T(8,128)S(1)}, s32[]{:T(128)}, f32[32,1]{0,1:T(1,128)S(1)}, f32[32,1,128,128]{3,2,1,0:T(8,128)}, ...), condition=%wide.region_4.5_spmd.clone, body=%wide.region_3.4_spmd.clone.sunk | while | flops 65540 | bytes 196733 | solution.py:21
  147.0 1.4 fusion.49
  167.3 1.4 fusion.49
  181.5 1.4 fusion.49
  185.5 1.4 fusion.49
  189.6 1.4 fusion.49
  212.2 2.2 fusion.7
  214.4 3.2 %multiply_reduce_fusion = (f32[8,256]{1,0:T(8,128)S(1)}, f32[8,1,128,256]{2,3,0,1:T(8,128)}) fusion(f32[8,128,256]{1,2,0:T(8,128)} %fusion.7, bf16[8,256,128]{2,1,0:T(8,128)(2,1)S(1)} %bitcast.101, bf16[8,256,128]{2,1,0:T(8,128)(2,1)S(1)} %bitcast.107, bf16[8,256,128]{2,1,0:T(8,128)(2,1)S(1)} %bitcast.103, f32[8,256]{1,0:T(8,128)S(1)} %get-tuple-element.129, ...), kind=kOutput, calls=%fused_computation.13 | convolution fusion | flops 271316992 | bytes 3751936 | tf_op jit(solution)/shard_map/nhts,nshd->nthd/dot_general | solution.py:52
  217.6 1.6 multiply_convert_fusion.1
  220.2 14.9 %all-to-all-start.4 = ((bf16[16,128,128]{1,2,0:T(8,128)(2,1)}), bf16[16,128,128]{1,2,0:T(8,128)(2,1)S(1)}, u32[]{:S(2)}, u32[]{:S(2)}) async-start(bf16[16,128,128]{1,2,0:T(8,128)(2,1)} %copy.55), calls=%async_computation.4 | async-start | bytes 1048576 | tf_op jit(solution)/shard_map/all_to_all | solution.py:97
  235.1 47.8 %all-gather.7.cloned.1.call-done = bf16[512,4,2048]{2,1,0:T(4,128)(2,1)} async-done(((bf16[1,4,2048]{2,1,0:T(4,128)(2,1)}), bf16[512,4,2048]{2,1,0:T(4,128)(2,1)}) %all-gather.7.cloned.1.call-update) | async-done | bytes 8388624 | tf_op jit(solution)/shard_map/all_gather | solution.py:100
  282.9 12.5 %reshape.334 = bf16[2048,2048]{1,0:T(8,128)(2,1)} reshape(bf16[512,4,2048]{2,1,0:T(4,128)(2,1)} %all-gather.7.cloned.1.call-done) | data formatting | bytes 16777216
  295.4 5.5 %convolution_convert_fusion = bf16[128,2048]{1,0:T(8,128)(2,1)} fusion(bf16[128,2048]{0,1:T(8,128)(2,1)S(1)} %bitcast.98, bf16[2048,2048]{1,0:T(8,128)(2,1)} %reshape.334), kind=kOutput, calls=%fused_computation.3 | convolution fusion | flops 1074003968 | bytes 9437184 | tf_op jit(solution)/shard_map/dot_general | solution.py:98
  (97 shorter events, 68.7 us)
Async XLA Ops:
  6.5 24.2 %copy-start = (bf16[128,2048]{1,0:T(8,128)(2,1)S(1)}, bf16[128,2048]{1,0:T(8,128)(2,1)}, u32[]{:S(2)}) copy-start(bf16[128,2048]{1,0:T(8,128)(2,1)} %param.9) | copy-start | bytes 1572868
  7.9 18.8 %all-to-all-start.2 = ((bf16[128,16,1]{0,2,1:T(2,128)(2,1)}), bf16[128,16,1]{0,2,1:T(2,128)(2,1)S(1)}, u32[]{:S(2)}, u32[]{:S(2)}) async-start(bf16[128,16,1]{0,2,1:T(2,128)(2,1)} %copy.47), calls=%async_computation.2 | async-start | bytes 16384 | tf_op jit(solution)/shard_map/all_to_all | solution.py:29
  26.7 21.3 %all-to-all-start.1 = ((bf16[128,16,128]{0,2,1:T(8,128)(2,1)}), bf16[128,16,128]{0,2,1:T(8,128)(2,1)S(1)}, u32[]{:S(2)}, u32[]{:S(2)}) async-start(bf16[128,16,128]{0,2,1:T(8,128)(2,1)} %bitcast.2), calls=%async_computation.1 | async-start | bytes 1048576 | tf_op jit(solution)/shard_map/all_to_all | solution.py:27
  32.4 39.3 %copy-start.1 = (bf16[128,2048]{1,0:T(8,128)(2,1)S(1)}, bf16[128,2048]{1,0:T(8,128)(2,1)}, u32[]{:S(2)}) copy-start(bf16[128,2048]{1,0:T(8,128)(2,1)} %param.7) | copy-start | bytes 1572868
  48.0 20.1 %all-to-all-start.3 = ((bf16[128,16,128]{2,0,1:T(8,128)(2,1)}), bf16[128,16,128]{2,0,1:T(8,128)(2,1)S(1)}, u32[]{:S(2)}, u32[]{:S(2)}) async-start(bf16[128,16,128]{2,0,1:T(8,128)(2,1)} %copy_bitcast_fusion), calls=%async_computation.3 | async-start | bytes 1048576 | tf_op jit(solution)/shard_map/all_to_all | solution.py:28
  51.5 94.9 %all-gather.5.cloned.1.call-start = ((), (), s32[]{:S(2)}) async-start(), calls=%async_computation.5 | async-start | bytes 2162688 | tf_op jit(solution)/shard_map/all_gather | solution.py:11
  70.9 211.9 %all-gather.7.cloned.1.call-start = ((), (), s32[]{:S(2)}) async-start(), calls=%async_computation.6 | async-start | bytes 8404992 | tf_op jit(solution)/shard_map/all_gather | solution.py:100
  72.6 139.6 %all-to-all-start = ((bf16[128,16,128]{2,0,1:T(8,128)(2,1)}), bf16[128,16,128]{2,0,1:T(8,128)(2,1)S(1)}, u32[]{:S(2)}, u32[]{:S(2)}) async-start(bf16[128,16,128]{2,0,1:T(8,128)(2,1)} %copy_bitcast_fusion.1), calls=%async_computation | async-start | bytes 1048576 | tf_op jit(solution)/shard_map/all_to_all | solution.py:26
  220.2 75.2 %all-to-all-start.4 = ((bf16[16,128,128]{1,2,0:T(8,128)(2,1)}), bf16[16,128,128]{1,2,0:T(8,128)(2,1)S(1)}, u32[]{:S(2)}, u32[]{:S(2)}) async-start(bf16[16,128,128]{1,2,0:T(8,128)(2,1)} %copy.55), calls=%async_computation.4 | async-start | bytes 1048576 | tf_op jit(solution)/shard_map/all_to_all | solution.py:97
Sparse Core Ops, SparseCore 0:
  71.1 75.2 all-gather.4
  150.9 131.8 all-gather.6
where the time goes:
time: 310 us; the launch traced here: 308 us
  waiting for transfers between devices  89.7 us (29%)
  blocking collectives  61.9 us (20%)
  other arithmetic  48.3 us (16%)
  local copies, waits for them, and re-layouts  41.1 us (13%)
  starting transfers between devices  37.7 us (12%)
  matrix products  14.5 us (5%)
  between operations  13.5 us (4%)
    unnamed x1, blocking collectives  61.9 us
    all_gather x1, waiting for transfers between devices, local(): lax.all_gather(out_weight, ('seq', 'head'), axis=0, tiled=True)  47.8 us
    select_n x32, other arithmetic, turn(): return jax.tree.map(lambda a, b: jnp.where(reached, a, b), new, before)  45.4 us
    exp x32, local copies, waits for them, and re-layouts, link(): jnp.exp(later[1])[:, None, None] * earlier[0] + later[0]  18.8 us
    unnamed x9, local copies, waits for them, and re-layouts  16.9 us
    all_to_all x1, waiting for transfers between devices, local(): lax.all_to_all(keys, 'head', split_axis=1, concat_axis=0, tiled=True)  15.6 us
    all_to_all x1, waiting for transfers between devices, local(): lax.all_to_all(values, 'head', split_axis=1, concat_axis=0, tiled=True)  15.1 us
    all_to_all x1, starting transfers between devices, local(): lax.all_to_all(normed, 'head', split_axis=0, concat_axis=1, tiled=True)  14.9 us
  transfers between devices with their start and end apart: 7, of which 5 were waited for; matrix products, arithmetic and copies ran while one was open for 31% of the time, Pallas kernels for 0%

commit v1 on v0

--- a/solution.py
+++ b/solution.py
@@ -4,6 +4,11 @@
 from jax.sharding import PartitionSpec as P
 
 SPAN = 256
+
+
+def gather_over(x, name, d):
+    repeated = jnp.stack([x] * lax.axis_size(name))
+    return jnp.concatenate(lax.all_to_all(repeated, name, 0, 0), axis=d)
 
 
 def entering(x, axis, combine, identity):
@@ -96,9 +101,7 @@
     normed = normed.reshape(shard_rows, head_count * head_dim)
     restored = lax.all_to_all(normed, "head", split_axis=0, concat_axis=1, tiled=True)
     projected = jnp.dot(
-        restored,
-        lax.all_gather(out_weight, ("seq", "head"), axis=0, tiled=True),
-        preferred_element_type=jnp.float32,
+        restored, gather_over(out_weight, ("seq", "head"), 0), preferred_element_type=jnp.float32
     )
     return projected.astype(jnp.bfloat16)
 

time: 310 us -> 482 us (1.55)
  blocking collectives: 61.9 us -> 254 us
  waiting for transfers between devices: 89.7 us -> 43.6 us
  starting transfers between devices: 37.7 us -> 57.3 us
  local copies, waits for them, and re-layouts: 41.1 us -> 47 us
    unnamed x1, blocking collectives: 61.9 us -> 234 us
    all_gather x1 -> x0, waiting for transfers between devices: 47.8 us -> none  [local(): lax.all_gather(out_weight, ('seq', 'head'), axis=0, tiled=True)]
    all_to_all x0 -> x1, blocking collectives: none -> 20 us  [local(): lax.all_to_all(values, 'head', split_axis=1, concat_axis=0, tiled=True)]
    all_to_all x1, waiting for transfers between devices: 0.01 us -> 16.3 us  [local(): lax.all_to_all(queries, 'head', split_axis=1, concat_axis=0, tiled=True)]
    all_to_all x1, waiting for transfers between devices: 15.1 us -> 0.01 us  [gather_over(): return jnp.concatenate(lax.all_to_all(repeated, name, 0, 0), axis=d)]
    unnamed x9 -> x12, local copies, waits for them, and re-layouts: 16.9 us -> 3.48 us
    reshape x0 -> x1, local copies, waits for them, and re-layouts: none -> 12.5 us  [gather_over(): return jnp.concatenate(lax.all_to_all(repeated, name, 0, 0), axis=d)]
    all_to_all x1, starting transfers between devices: 3.47 us -> 15.4 us  [gather_over(): return jnp.concatenate(lax.all_to_all(repeated, name, 0, 0), axis=d)]
  transfers between devices with their start and end apart: 7 -> 6, of which waited for: 5 -> 4; matrix products, arithmetic and copies ran while one was open for 31% -> 20% of each run, Pallas kernels for 0% -> 0%
where the time goes in v1:
time: 482 us; the launch traced here: 479 us
  blocking collectives  254 us (53%)
  starting transfers between devices  57.3 us (12%)
  other arithmetic  49.8 us (10%)
  local copies, waits for them, and re-layouts  47 us (10%)
  waiting for transfers between devices  43.6 us (9%)
  between operations  13.6 us (3%)
  matrix products  13.5 us (3%)
    unnamed x1, blocking collectives  234 us
    select_n x32, other arithmetic, turn(): return jax.tree.map(lambda a, b: jnp.where(reached, a, b), new, before)  48.1 us
    all_to_all x1, starting transfers between devices, local(): lax.all_to_all(normed, 'head', split_axis=0, concat_axis=1, tiled=True)  22.6 us
    all_to_all x1, blocking collectives, local(): lax.all_to_all(values, 'head', split_axis=1, concat_axis=0, tiled=True)  20 us
    exp x32, local copies, waits for them, and re-layouts, link(): jnp.exp(later[1])[:, None, None] * earlier[0] + later[0]  18.9 us
    all_to_all x1, waiting for transfers between devices, local(): lax.all_to_all(keys, 'head', split_axis=1, concat_axis=0, tiled=True)  16.5 us
    all_to_all x1, waiting for transfers between devices, local(): lax.all_to_all(queries, 'head', split_axis=1, concat_axis=0, tiled=True)  16.3 us
    all_to_all x1, starting transfers between devices, gather_over(): return jnp.concatenate(lax.all_to_all(repeated, name, 0, 0), axis=d)  15.4 us
  transfers between devices with their start and end apart: 6, of which 4 were waited for; matrix products, arithmetic and copies ran while one was open for 20% of the time, Pallas kernels for 0%

profile of v1, /device:TPU:1, one launch (start us, length us, event | category | flops | bytes accessed | tf_op | source)
XLA Modules:
  0.0 479.4 jit_solution(7149954915545224031)
XLA Ops:
  7.9 11.8 %all-to-all-start.2 = ((bf16[128,16,1]{0,2,1:T(2,128)(2,1)}), bf16[128,16,1]{0,2,1:T(2,128)(2,1)S(1)}, u32[]{:S(2)}, u32[]{:S(2)}) async-start(bf16[128,16,1]{0,2,1:T(2,128)(2,1)} %copy.47), calls=%async_computation.2 | async-start | bytes 16384 | tf_op jit(solution)/shard_map/all_to_all | solution.py:34
  20.7 6.1 %all-to-all-done.2 = bf16[128,16,1]{0,2,1:T(2,128)(2,1)S(1)} async-done(((bf16[128,16,1]{0,2,1:T(2,128)(2,1)}), bf16[128,16,1]{0,2,1:T(2,128)(2,1)S(1)}, u32[]{:S(2)}, u32[]{:S(2)}) %all-to-all-start.2) | async-done | bytes 4128 | tf_op jit(solution)/shard_map/all_to_all | solution.py:34
  26.8 4.0 all-to-all-start
  31.8 16.3 %all-to-all-done = bf16[128,16,128]{2,0,1:T(8,128)(2,1)S(1)} async-done(((bf16[128,16,128]{2,0,1:T(8,128)(2,1)}), bf16[128,16,128]{2,0,1:T(8,128)(2,1)S(1)}, u32[]{:S(2)}, u32[]{:S(2)}) %all-to-all-start) | async-done | bytes 524320 | tf_op jit(solution)/shard_map/all_to_all | solution.py:31
  48.1 3.5 all-to-all-start.1
  51.7 16.5 %all-to-all-done.1 = bf16[128,16,128]{0,2,1:T(8,128)(2,1)S(1)} async-done(((bf16[128,16,128]{0,2,1:T(8,128)(2,1)}), bf16[128,16,128]{0,2,1:T(8,128)(2,1)S(1)}, u32[]{:S(2)}, u32[]{:S(2)}) %all-to-all-start.1) | async-done | bytes 524320 | tf_op jit(solution)/shard_map/all_to_all | solution.py:32
  68.2 20.0 %all_to_all.85 = bf16[128,16,128]{2,0,1:T(8,128)(2,1)S(1)} all-to-all(bf16[128,16,128]{2,0,1:T(8,128)(2,1)S(1)} %copy_bitcast_fusion), channel_id=1, replica_groups=mesh['seq'=32,'head'=16] {'head'}, dimensions={1} | all-to-all | bytes 1048576 | tf_op jit(solution)/shard_map/all_to_all | solution.py:33
  88.2 7.5 %stack.2 = bf16[512,4,2048]{2,1,0:T(4,128)(2,1)} broadcast(bf16[4,2048]{1,0:T(4,128)(2,1)S(1)} %copy-done.3), dimensions={1,2} | broadcast | bytes 8404992 | tf_op jit(solution)/shard_map/stack | solution.py:10
  95.7 15.4 %all-to-all-start.5 = ((bf16[512,4,2048]{2,1,0:T(4,128)(2,1)}), bf16[512,4,2048]{2,1,0:T(4,128)(2,1)}, u32[]{:S(2)}, u32[]{:S(2)}) async-start(bf16[512,4,2048]{2,1,0:T(4,128)(2,1)} %stack.2), calls=%async_computation.5 | async-start | bytes 16777216 | tf_op jit(solution)/shard_map/all_to_all | solution.py:11
  114.2 2.0 fusion.18
  118.8 233.8 %all-reduce = f32[32]{0:T(128)S(1)} all-reduce(f32[32]{0:T(128)S(1)} %bitcast_dynamic-update-slice_fusion), channel_id=1, replica_groups=mesh['seq'=32,'head'=16] {'seq'}, use_global_device_ids=true, to_apply=%add | all-reduce | flops 32 | bytes 256
  352.9 67.8 %while.14 = (s32[]{:T(128)}, f32[1,128,128]{2,1,0:T(8,128)S(1)}, s32[]{:T(128)}, f32[32,1]{0,1:T(1,128)S(1)}, f32[32,1,128,128]{3,2,1,0:T(8,128)}, /*index=5*/s32[]{:T(128)}, s32[]{:T(128)}) while((s32[]{:T(128)}, f32[1,128,128]{2,1,0:T(8,128)S(1)}, s32[]{:T(128)}, f32[32,1]{0,1:T(1,128)S(1)}, f32[32,1,128,128]{3,2,1,0:T(8,128)}, ...), condition=%wide.region_4.5_spmd.clone, body=%wide.region_3.4_spmd.clone.sunk | while | flops 65540 | bytes 196733 | solution.py:26
  353.5 1.5 fusion.49
  355.6 1.5 fusion.49
  359.8 1.5 fusion.49
  361.9 1.5 fusion.49
  364.1 1.5 fusion.49
  366.2 1.5 fusion.49
  421.6 2.1 fusion.7
  423.7 2.2 multiply_reduce_fusion
  427.3 22.6 %all-to-all-start.4 = ((bf16[16,128,128]{1,2,0:T(8,128)(2,1)}), bf16[16,128,128]{1,2,0:T(8,128)(2,1)S(1)}, u32[]{:S(2)}, u32[]{:S(2)}) async-start(bf16[16,128,128]{1,2,0:T(8,128)(2,1)} %copy.55), calls=%async_computation.4 | async-start | bytes 1048576 | tf_op jit(solution)/shard_map/all_to_all | solution.py:102
  449.8 12.5 %reshape.333 = bf16[2048,2048]{1,0:T(8,128)(2,1)} reshape(bf16[512,4,2048]{2,1,0:T(4,128)(2,1)} %all-to-all-done.5) | data formatting | bytes 16777216 | tf_op jit(solution)/shard_map/reshape | solution.py:11
  462.3 4.7 all-to-all-done.4
  467.1 5.5 %convolution_convert_fusion = bf16[128,2048]{1,0:T(8,128)(2,1)} fusion(bf16[128,2048]{0,1:T(8,128)(2,1)S(1)} %bitcast.97, bf16[2048,2048]{1,0:T(8,128)(2,1)} %reshape.333), kind=kOutput, calls=%fused_computation.3 | convolution fusion | flops 1074003968 | bytes 9437184 | tf_op jit(solution)/shard_map/dot_general | solution.py:103
  (100 shorter events, 69.6 us)
Async XLA Ops:
  6.5 13.2 %copy-start = (bf16[128,2048]{1,0:T(8,128)(2,1)S(1)}, bf16[128,2048]{1,0:T(8,128)(2,1)}, u32[]{:S(2)}) copy-start(bf16[128,2048]{1,0:T(8,128)(2,1)} %param.7) | copy-start | bytes 1572868
  6.5 24.3 %copy-start.1 = (bf16[128,2048]{1,0:T(8,128)(2,1)S(1)}, bf16[128,2048]{1,0:T(8,128)(2,1)}, u32[]{:S(2)}) copy-start(bf16[128,2048]{1,0:T(8,128)(2,1)} %param.8) | copy-start | bytes 1572868
  7.9 18.9 %all-to-all-start.2 = ((bf16[128,16,1]{0,2,1:T(2,128)(2,1)}), bf16[128,16,1]{0,2,1:T(2,128)(2,1)S(1)}, u32[]{:S(2)}, u32[]{:S(2)}) async-start(bf16[128,16,1]{0,2,1:T(2,128)(2,1)} %copy.47), calls=%async_computation.2 | async-start | bytes 16384 | tf_op jit(solution)/shard_map/all_to_all | solution.py:34
  19.7 31.8 %copy-start.2 = (bf16[128,2048]{1,0:T(8,128)(2,1)S(1)}, bf16[128,2048]{1,0:T(8,128)(2,1)}, u32[]{:S(2)}) copy-start(bf16[128,2048]{1,0:T(8,128)(2,1)} %param.9) | copy-start | bytes 1572868
  26.8 21.3 %all-to-all-start = ((bf16[128,16,128]{2,0,1:T(8,128)(2,1)}), bf16[128,16,128]{2,0,1:T(8,128)(2,1)S(1)}, u32[]{:S(2)}, u32[]{:S(2)}) async-start(bf16[128,16,128]{2,0,1:T(8,128)(2,1)} %copy_bitcast_fusion.1), calls=%async_computation | async-start | bytes 1048576 | tf_op jit(solution)/shard_map/all_to_all | solution.py:31
  30.8 57.4 %copy-start.3 = (bf16[4,2048]{1,0:T(4,128)(2,1)S(1)}, bf16[4,2048]{1,0:T(4,128)(2,1)}, u32[]{:S(2)}) copy-start(bf16[4,2048]{1,0:T(4,128)(2,1)} %param.11) | copy-start | bytes 49156
  48.1 20.1 %all-to-all-start.1 = ((bf16[128,16,128]{0,2,1:T(8,128)(2,1)}), bf16[128,16,128]{0,2,1:T(8,128)(2,1)S(1)}, u32[]{:S(2)}, u32[]{:S(2)}) async-start(bf16[128,16,128]{0,2,1:T(8,128)(2,1)} %bitcast.2), calls=%async_computation.1 | async-start | bytes 1048576 | tf_op jit(solution)/shard_map/all_to_all | solution.py:32
  95.7 331.6 %all-to-all-start.5 = ((bf16[512,4,2048]{2,1,0:T(4,128)(2,1)}), bf16[512,4,2048]{2,1,0:T(4,128)(2,1)}, u32[]{:S(2)}, u32[]{:S(2)}) async-start(bf16[512,4,2048]{2,1,0:T(4,128)(2,1)} %stack.2), calls=%async_computation.5 | async-start | bytes 16777216 | tf_op jit(solution)/shard_map/all_to_all | solution.py:11
  111.1 241.8 %all-gather.3.cloned.1.call-start = ((), (), s32[]{:S(2)}) async-start(), calls=%async_computation.6 | async-start | bytes 2162688 | tf_op jit(solution)/shard_map/all_gather | solution.py:16
  427.3 39.8 %all-to-all-start.4 = ((bf16[16,128,128]{1,2,0:T(8,128)(2,1)}), bf16[16,128,128]{1,2,0:T(8,128)(2,1)S(1)}, u32[]{:S(2)}, u32[]{:S(2)}) async-start(bf16[16,128,128]{1,2,0:T(8,128)(2,1)} %copy.55), calls=%async_computation.4 | async-start | bytes 1048576 | tf_op jit(solution)/shard_map/all_to_all | solution.py:102
Sparse Core Ops, SparseCore 0:
  116.4 99.9 all-gather.2
